TPU v7x, 32 devices: a whole 2x2x4 slice. The times are simulated.
32 devices in a mesh: dp: 2 (over x), seq: 8 (over z, core), tensor: 2 (over y).
Axes of the slice: x: 2, y: 2, z: 4, core: 2. Of those that a mesh axis runs over, the one named last changes fastest.
Arguments:
- events: bfloat16 [4, 2048, 1536], P('dp', 'seq', 'tensor'), may hold values from -6 to 6
- gate_in: bfloat16 [4, 2048, 1536], P('dp', 'seq', 'tensor'), may hold values from -6 to 6
- filters: bfloat16 [1024, 1536], P(None, 'tensor'), may hold values from -0.1875 to 0.1875
- proj: bfloat16 [1536, 1536], P('tensor'), may hold values from -0.15625 to 0.15625
- lengths: int32 [4], P('dp'), may hold values from 256 to 2048, as said below
- cotangent: bfloat16 [4, 2048, 1536], P('dp', 'seq', 'tensor'), may hold values from -6 to 6
Outputs:
- mixed: bfloat16 [4, 2048, 1536], P('dp', 'seq', 'tensor')
- grad_input: bfloat16 [4, 2048, 1536], P('dp', 'seq', 'tensor')
- grad_gate: bfloat16 [4, 2048, 1536], P('dp', 'seq', 'tensor')
- grad_filters: float32 [1024, 1536], P(None, 'tensor')
- grad_proj: float32 [1536, 1536], P('tensor')
Inputs may be any that keep to these rules, and one draw needn't show every extreme that they name: `lengths`: each length is a multiple of 256, and some user's length is 2048.
All inputs are finite; a program needn't handle non-finite values.
Results may differ from a plain program's by a relative error of at most 0.0049.
Values may be sent and summed in bfloat16 or wider, within the bound.
No kernel may reach another device: no remote copies, remote signals or barrier semaphores. Data moves between devices by JAX's collectives and lax.ppermute only.
A program may use at most 128 MiB of HBM per device.

v0:
```python
import math

import jax
import jax.numpy as jnp
from jax import lax
from jax.sharding import PartitionSpec as P


def shifted(value, axis, by):
    count = lax.axis_size(axis)
    pairs = [(i, i + by) for i in range(count) if 0 <= i + by < count]
    return lax.ppermute(value, axis, pairs)


def depthwise(lhs, kernel):
    return lax.conv_general_dilated(
        lhs,
        kernel[:, None, :],
        (1,),
        "VALID",
        dimension_numbers=("NWC", "WIO", "NWC"),
        feature_group_count=lhs.shape[2],
        preferred_element_type=jnp.float32,
    )


def filter_grad(window, grad_conv):
    users, width, chans = window.shape
    length = grad_conv.shape[1]
    lhs = jnp.transpose(window, (1, 0, 2)).reshape(1, width, users * chans)
    kernel = jnp.transpose(grad_conv, (1, 0, 2)).reshape(length, users * chans)
    result = depthwise(lhs, kernel)
    return jnp.sum(result.reshape(-1, users, chans), axis=1)[::-1]


def shards(events, gate_in, filters, proj, lengths, cotangent):
    users, block_len, chans = events.shape
    taps_len = filters.shape[0]
    reach = taps_len // block_len
    first = lax.axis_index("seq") * block_len
    position = first + jnp.arange(block_len, dtype=jnp.int32)
    live = (position[None, :] < lengths[:, None]).astype(jnp.float32)[:, :, None]
    masked = (events.astype(jnp.float32) * live).astype(jnp.bfloat16)
    earlier = []
    for offset in range(1, reach + 1):
        earlier.append(shifted(masked, "seq", offset))
    window = jnp.concatenate(earlier[::-1] + [masked], axis=1)[:, 1:]
    conv = depthwise(window, filters[::-1])
    gate_f = gate_in.astype(jnp.float32)
    gate_sig = jax.nn.sigmoid(gate_f)
    silu_g = gate_f * gate_sig
    gated = (silu_g * conv * live).astype(jnp.bfloat16)
    gated_rows = gated.reshape(-1, chans)
    partial_out = jnp.dot(gated_rows, proj, preferred_element_type=jnp.float32)
    out_rows = lax.psum_scatter(partial_out, "tensor", scatter_dimension=1, tiled=True)
    mixed = out_rows.astype(jnp.bfloat16).reshape(users, block_len, chans)
    cot_rows = cotangent.reshape(-1, chans)
    piece = lax.all_gather(cot_rows, "tensor", axis=1, tiled=True)
    grad_acc = lax.dot_general(
        piece, proj, (((1,), (1,)), ((), ())), preferred_element_type=jnp.float32
    )
    outer = lax.dot_general(
        gated_rows, piece, (((0,), (0,)), ((), ())), preferred_element_type=jnp.float32
    )
    grad_gated = grad_acc.reshape(users, block_len, chans) * live
    grad_conv = (grad_gated * silu_g).astype(jnp.bfloat16)
    grad_gate = (grad_gated * conv * gate_sig * (1.0 + gate_f * (1.0 - gate_sig))).astype(
        jnp.bfloat16
    )
    following = [grad_conv]
    for offset in range(1, reach + 1):
        following.append(shifted(grad_conv, "seq", -offset))
    ahead = jnp.concatenate(following, axis=1)[:, : block_len + taps_len - 1]
    grad_input = (depthwise(ahead, filters) * live).astype(jnp.bfloat16)
    filter_local = filter_grad(window, grad_conv)
    filter_sum, proj_sum = lax.psum((filter_local, outer), ("dp", "seq"))
    scale = 1.0 / math.sqrt(users * lax.axis_size("dp") * block_len * lax.axis_size("seq"))
    return (mixed, grad_input, grad_gate, filter_sum * scale, proj_sum * scale)


def solution(mesh):
    in_specs = (
        P("dp", "seq", "tensor"),
        P("dp", "seq", "tensor"),
        P(None, "tensor"),
        P("tensor", None),
        P("dp"),
        P("dp", "seq", "tensor"),
    )
    out_specs = (
        P("dp", "seq", "tensor"),
        P("dp", "seq", "tensor"),
        P("dp", "seq", "tensor"),
        P(None, "tensor"),
        P("tensor", None),
    )
    return jax.shard_map(shards, mesh=mesh, in_specs=in_specs, out_specs=out_specs, check_vma=False)
```

profile of v0, /device:TPU:0, one launch (start us, length us, event | category | flops | bytes accessed | tf_op | source)
XLA Modules:
  0.0 1037.7 jit_solution(3310441541021366550)
XLA Ops:
  7.2 0.0 all-gather.2.cloned.1.call-start
  7.2 0.9 compare_convert_fusion
  8.1 1.3 multiply_convert_fusion.2
  9.5 6.9 collective-permute-start
  16.3 3.6 collective-permute-start.1
  19.9 3.0 collective-permute-start.2
  22.9 2.2 collective-permute-start.3
  25.1 0.0 all-gather.2.cloned.1.call-update
  25.1 0.0 all-reduce.3.cloned.1.call-start
  25.1 23.0 %rev.6 = bf16[1024,768]{1,0:T(8,128)(2,1)} reverse(bf16[1024,768]{1,0:T(8,128)(2,1)} %param.8), dimensions={0} | reverse | bytes 3145728 | tf_op jit(solution)/shard_map/rev | solution.py:48
  48.2 1.2 constant_dynamic-update-slice_fusion.4
  49.4 0.9 collective-permute-done.1
  50.2 1.2 constant_dynamic-update-slice_fusion.3
  51.4 15.7 %collective-permute-done.2 = bf16[2,256,768]{2,1,0:T(8,128)(2,1)} collective-permute-done((bf16[2,256,768]{2,1,0:T(8,128)(2,1)S(1)}, bf16[2,256,768]{2,1,0:T(8,128)(2,1)}, u32[]{:S(2)}, u32[]{:S(2)}) %collective-permute-start.2) | collective-permute-done | bytes 786464 | tf_op jit(solution)/shard_map/ppermute | solution.py:12
  67.1 1.2 constant_dynamic-update-slice_fusion.2
  68.3 1.2 constant_dynamic-update-slice_fusion.1
  69.5 0.2 constant_dynamic-update-slice_fusion
  69.7 224.4 %fusion.2 = f32[2,256,768]{2,0,1:T(2,128)} fusion(bf16[2,1280,768]{2,1,0:T(8,128)(2,1)S(1)} %constant_dynamic-update-slice_fusion, bf16[1024,1,768]{2,0,1:T(8,128)(2,1)S(1)} %bitcast.26), kind=kOutput, calls=%fused_computation.3 | convolution fusion | flops 805306368 | bytes 7077888 | tf_op jit(solution)/shard_map/conv_general_dilated | solution.py:16
  294.1 3.0 slice_bitcast_fusion
  297.1 6.3 copy.43
  303.3 16.7 %copy.45 = bf16[1,1279,1536]{2,0,1:T(2,128)(2,1)} copy(bf16[1,1279,1536]{1,2,0:T(8,128)(2,1)} %bitcast.19) | data formatting | bytes 7858176 | tf_op jit(solution)/shard_map/reshape | solution.py:30
  320.0 2.9 fusion.14
  322.9 1.2 copy-done.1
  324.1 1.6 constant_dynamic-update-slice_fusion.9
  325.7 1.3 collective-permute-start.4
  327.0 1.3 collective-permute-start.5
  328.3 1.3 collective-permute-start.6
  329.6 1.3 collective-permute-start.7
  330.9 1.4 copy.44
  332.3 2.9 copy.46
  335.3 193.2 %convolution_reduce_fusion = f32[1024,1536]{1,0:T(8,128)} fusion(bf16[1,1279,1536]{2,0,1:T(2,128)(2,1)} %copy.45, bf16[256,1,1536]{2,1,0:T(2,128)(2,1)} %copy.46), kind=kOutput, calls=%fused_computation.23 | convolution fusion | flops 805306368 | bytes 11006976 | tf_op jit(solution)/shard_map/conv_general_dilated | solution.py:16
  528.4 8.3 reshape.66
  536.7 11.9 %reduce_sum.9 = f32[1024,768]{1,0:T(8,128)} reduce(f32[1024,2,768]{2,1,0:T(2,128)} %reshape.66, f32[]{:T(128)} %constant.19.clone.1), dimensions={1}, to_apply=%region_1.0 | reduce | flops 786432 | bytes 9437188 | tf_op jit(solution)/shard_map/reduce_sum | solution.py:33
  548.6 24.7 %rev.7 = f32[1024,768]{1,0:T(8,128)} reverse(f32[1024,768]{1,0:T(8,128)} %reduce_sum.9), dimensions={0} | reverse | bytes 6291456 | tf_op jit(solution)/shard_map/rev | solution.py:33
  573.3 2.1 constant_dynamic-update-slice_fusion.8
  575.4 2.2 constant_dynamic-update-slice_fusion.7
  577.6 2.1 constant_dynamic-update-slice_fusion.6
  579.6 2.1 constant_dynamic-update-slice_fusion.5
  581.7 195.2 %fusion = f32[2,256,768]{2,0,1:T(2,128)S(1)} fusion(bf16[2,1280,768]{2,1,0:T(8,128)(2,1)} %constant_dynamic-update-slice_fusion.5, bf16[1024,1,768]{2,0,1:T(8,128)(2,1)S(1)} %bitcast.25), kind=kOutput, calls=%fused_computation.1 | convolution fusion | flops 805306368 | bytes 7077888 | tf_op jit(solution)/shard_map/conv_general_dilated | solution.py:16
  777.0 2.1 fusion.11
  779.1 3.6 fusion.15
  782.7 0.0 reduce-scatter.2.cloned.1.call-start
  782.8 3.1 fusion.13
  785.9 196.6 %all-reduce.3.cloned.1.call-done = (f32[1024,768]{1,0:T(8,128)}, f32[768,1536]{1,0:T(8,128)}) async-done(((f32[1024,768]{1,0:T(8,128)}, f32[768,1536]{1,0:T(8,128)}), (f32[1024,768]{1,0:T(8,128)}, f32[768,1536]{1,0:T(8,128)})) %all-reduce.3.cloned.1.call-update) | async-done | bytes 7864336 | tf_op jit(solution)/shard_map/psum | solution.py:76
  982.6 4.0 broadcast_multiply_fusion.1
  986.6 2.7 broadcast_multiply_fusion
  989.3 39.1 %reduce-scatter.2.cloned.1.call-done = f32[512,768]{1,0:T(8,128)} async-done(((f32[512,1536]{1,0:T(8,128)}), f32[512,768]{1,0:T(8,128)}) %reduce-scatter.2.cloned.1.call-update) | async-done | bytes 1572880 | tf_op jit(solution)/shard_map/reduce_scatter | solution.py:55
  1028.4 2.4 convert_element_type.36
  (37 shorter events, 0.1 us)
Async XLA Ops:
  7.2 312.9 %copy-start = (bf16[768,1536]{1,0:T(8,128)(2,1)S(1)}, bf16[768,1536]{1,0:T(8,128)(2,1)}, u32[]{:S(2)}) copy-start(bf16[768,1536]{1,0:T(8,128)(2,1)} %param.9) | copy-start | bytes 7077892
  7.2 312.8 %all-gather.2.cloned.1.call-start = ((), (), s32[]{:S(2)}) async-start(), calls=%async_computation.2 | async-start | bytes 2359296 | tf_op jit(solution)/shard_map/all_gather | solution.py:58
  8.1 61.4 %copy-start.11 = (f32[2,256]{1,0:T(2,128)}, f32[2,256]{1,0:T(2,128)S(1)}, u32[]{:S(2)}) copy-start(f32[2,256]{1,0:T(2,128)S(1)} %compare_convert_fusion) | copy-start | bytes 6148
  9.5 38.7 %collective-permute-start = (bf16[2,256,768]{2,1,0:T(8,128)(2,1)S(1)}, bf16[2,256,768]{2,1,0:T(8,128)(2,1)}, u32[]{:S(2)}, u32[]{:S(2)}) collective-permute-start(bf16[2,256,768]{2,1,0:T(8,128)(2,1)S(1)} %multiply_convert_fusion.2), channel_id=1, source_target_pairs={{0,8},{2,10},{4,12},{6,14},{1,9},{3,11},{5,13},{7,15},{16,24},{18,... | collective-permute-start | bytes 2359304 | tf_op jit(solution)/shard_map/ppermute | solution.py:12
  16.3 33.9 %collective-permute-start.1 = (bf16[2,256,768]{2,1,0:T(8,128)(2,1)S(1)}, bf16[2,256,768]{2,1,0:T(8,128)(2,1)}, u32[]{:S(2)}, u32[]{:S(2)}) collective-permute-start(bf16[2,256,768]{2,1,0:T(8,128)(2,1)S(1)} %multiply_convert_fusion.2), channel_id=1, source_target_pairs={{0,6},{2,8},{4,10},{6,12},{8,14},{1,7},{3,9},{5,11},{7,13},{9,15},... | collective-permute-start | bytes 2359304 | tf_op jit(solution)/shard_map/ppermute | solution.py:12
  19.9 47.2 %collective-permute-start.2 = (bf16[2,256,768]{2,1,0:T(8,128)(2,1)S(1)}, bf16[2,256,768]{2,1,0:T(8,128)(2,1)}, u32[]{:S(2)}, u32[]{:S(2)}) collective-permute-start(bf16[2,256,768]{2,1,0:T(8,128)(2,1)S(1)} %multiply_convert_fusion.2), channel_id=1, source_target_pairs={{0,4},{2,6},{4,8},{6,10},{8,12},{10,14},{1,5},{3,7},{5,9},{7,11},{... | collective-permute-start | bytes 2359304 | tf_op jit(solution)/shard_map/ppermute | solution.py:12
  22.9 45.4 %collective-permute-start.3 = (bf16[2,256,768]{2,1,0:T(8,128)(2,1)S(1)}, bf16[2,256,768]{2,1,0:T(8,128)(2,1)}, u32[]{:S(2)}, u32[]{:S(2)}) collective-permute-start(bf16[2,256,768]{2,1,0:T(8,128)(2,1)S(1)} %multiply_convert_fusion.2), channel_id=1, source_target_pairs={{0,2},{2,4},{4,6},{6,8},{8,10},{10,12},{12,14},{1,3},{3,5},{5,7},{... | collective-permute-start | bytes 2359304 | tf_op jit(solution)/shard_map/ppermute | solution.py:12
  25.1 957.5 %all-reduce.3.cloned.1.call-start = ((), (), s32[]{:S(2)}) async-start(), calls=%async_computation.3 | async-start | bytes 15728640 | tf_op jit(solution)/shard_map/psum | solution.py:76
  49.3 20.1 %copy-start.6 = (bf16[2,256,768]{2,1,0:T(8,128)(2,1)S(1)}, bf16[2,256,768]{2,1,0:T(8,128)(2,1)}, u32[]{:S(2)}) copy-start(bf16[2,256,768]{2,1,0:T(8,128)(2,1)} %param.6) | copy-start | bytes 2359300
  51.4 18.3 %copy-start.9 = (bf16[1024,768]{1,0:T(8,128)(2,1)S(1)}, bf16[1024,768]{1,0:T(8,128)(2,1)}, u32[]{:S(2)}) copy-start(bf16[1024,768]{1,0:T(8,128)(2,1)} %rev.6) | copy-start | bytes 4718596
  320.0 4.1 copy-start.4
  320.0 4.1 copy-start.12
  322.9 1.2 copy-start.1
  325.7 247.6 %collective-permute-start.4 = (bf16[2,256,768]{2,1,0:T(8,128)(2,1)}, bf16[2,256,768]{2,1,0:T(8,128)(2,1)}, u32[]{:S(2)}, u32[]{:S(2)}) collective-permute-start(bf16[2,256,768]{2,1,0:T(8,128)(2,1)} %get-tuple-element.18), channel_id=1, source_target_pairs={{2,0},{4,2},{6,4},{8,6},{10,8},{12,10},{14,12},{3,1},{5,3},{7,5},{... | collective-permute-start | bytes 2359304 | tf_op jit(solution)/shard_map/ppermute | solution.py:12
  327.0 248.4 %collective-permute-start.5 = (bf16[2,256,768]{2,1,0:T(8,128)(2,1)}, bf16[2,256,768]{2,1,0:T(8,128)(2,1)}, u32[]{:S(2)}, u32[]{:S(2)}) collective-permute-start(bf16[2,256,768]{2,1,0:T(8,128)(2,1)} %get-tuple-element.18), channel_id=1, source_target_pairs={{4,0},{6,2},{8,4},{10,6},{12,8},{14,10},{5,1},{7,3},{9,5},{11,7},{... | collective-permute-start | bytes 2359304 | tf_op jit(solution)/shard_map/ppermute | solution.py:12
  328.3 249.2 %collective-permute-start.6 = (bf16[2,256,768]{2,1,0:T(8,128)(2,1)}, bf16[2,256,768]{2,1,0:T(8,128)(2,1)}, u32[]{:S(2)}, u32[]{:S(2)}) collective-permute-start(bf16[2,256,768]{2,1,0:T(8,128)(2,1)} %get-tuple-element.18), channel_id=1, source_target_pairs={{6,0},{8,2},{10,4},{12,6},{14,8},{7,1},{9,3},{11,5},{13,7},{15,9},... | collective-permute-start | bytes 2359304 | tf_op jit(solution)/shard_map/ppermute | solution.py:12
  329.6 250.0 %collective-permute-start.7 = (bf16[2,256,768]{2,1,0:T(8,128)(2,1)}, bf16[2,256,768]{2,1,0:T(8,128)(2,1)}, u32[]{:S(2)}, u32[]{:S(2)}) collective-permute-start(bf16[2,256,768]{2,1,0:T(8,128)(2,1)} %get-tuple-element.18), channel_id=1, source_target_pairs={{8,0},{10,2},{12,4},{14,6},{9,1},{11,3},{13,5},{15,7},{24,16},{26,... | collective-permute-start | bytes 2359304 | tf_op jit(solution)/shard_map/ppermute | solution.py:12
  575.4 6.3 copy-start.8
  581.7 195.3 %copy-start.2 = (f32[512,768]{1,0:T(8,128)S(1)}, f32[512,768]{1,0:T(8,128)}, u32[]{:S(2)}) copy-start(f32[512,768]{1,0:T(8,128)} %copy-done.1) | copy-start | bytes 4718596
  581.7 195.3 %copy-start.5 = (bf16[2,256,768]{2,1,0:T(8,128)(2,1)S(1)}, bf16[2,256,768]{2,1,0:T(8,128)(2,1)}, u32[]{:S(2)}) copy-start(bf16[2,256,768]{2,1,0:T(8,128)(2,1)} %param.7) | copy-start | bytes 2359300
  581.7 195.3 %copy-start.10 = (f32[2,256,768]{2,0,1:T(2,128)S(1)}, f32[2,256,768]{2,0,1:T(2,128)}, u32[]{:S(2)}) copy-start(f32[2,256,768]{2,0,1:T(2,128)} %fusion.2) | copy-start | bytes 4718596
  581.7 195.3 %copy-start.13 = (f32[2,256]{1,0:T(2,128)S(1)}, f32[2,256]{1,0:T(2,128)}, u32[]{:S(2)}) copy-start(f32[2,256]{1,0:T(2,128)} %copy-done.11) | copy-start | bytes 6148
  777.0 2.1 copy-start.7
  782.7 245.6 %reduce-scatter.2.cloned.1.call-start = ((), (), s32[]{:S(2)}) async-start(), calls=%async_computation.1 | async-start | bytes 4718592 | tf_op jit(solution)/shard_map/reduce_scatter | solution.py:55
  982.6 4.0 copy-start.3
Sparse Core Ops, SparseCore 0:
  25.2 25.3 all-gather.1
  782.9 199.6 all-reduce.2
  984.8 43.4 reduce-scatter.1
where the time goes:
time: 1050 us; the launch traced here: 1040 us
  matrix products  622 us (59%)
  waiting for transfers between devices  252 us (24%)
  local copies, waits for them, and re-layouts  101 us (10%)
  other arithmetic  27.1 us (3%)
  starting transfers between devices  20.9 us (2%)
  between operations  14.4 us (1%)
    conv_general_dilated x3, matrix products, depthwise(): lax.conv_general_dilated(lhs, kernel[:, None, :], (1,), 'VALID', dimensio...  613 us
    psum x1, waiting for transfers between devices, shards(): filter_sum, proj_sum = lax.psum((filter_local, outer), ('dp', 'seq'))  197 us
    reduce_scatter x1, waiting for transfers between devices, shards(): lax.psum_scatter(partial_out, 'tensor', scatter_dimension=1, tiled=True)  39.1 us
    rev x1, local copies, waits for them, and re-layouts, filter_grad(): return jnp.sum(result.reshape(-1, users, chans), axis=1)[::-1]  24.7 us
    rev x1, local copies, waits for them, and re-layouts, shards(): conv = depthwise(window, filters[::-1])  23 us
  transfers between devices with their start and end apart: 11, of which 4 were waited for; matrix products, arithmetic and copies ran while one was open for 52% of the time, Pallas kernels for 0%

commit v1 on v0

v1 whole, which is shorter than its diff:
```python
import functools
import math

import jax
import jax.numpy as jnp
import numpy as np
from jax import lax
from jax.experimental import pallas as pl
from jax.experimental.pallas import tpu as pltpu
from jax.sharding import PartitionSpec as P

F32 = jnp.float32
BF16 = jnp.bfloat16


def tables(block):
    size = 2 * block
    freq = np.concatenate([np.arange(0, block, 2), np.arange(1, block, 2)])
    turn = ((2 * freq[:, None] + 1) * np.arange(block)[None, :]) % (2 * size)
    angle = turn * (np.pi / size)
    full = np.concatenate([np.cos(angle), np.sin(angle)], axis=0)
    inv = full.T / block

    def pair(table):
        high = table.astype(jnp.bfloat16)
        low = (table - high.astype(np.float64)).astype(jnp.bfloat16)
        return high, low

    fwd = np.concatenate(pair(full), axis=1)
    inv_high, inv_low = pair(inv)
    return fwd, np.concatenate([inv_high, inv_high, inv_low], axis=1)


def forward(tab_ref, block):
    twice = jnp.concatenate([block, block], axis=0)
    return jnp.dot(tab_ref[...], twice, preferred_element_type=F32)


def backward(inv_ref, z_ref, at, size):
    both = jnp.dot(inv_ref[:, : 2 * size], z_ref[at], preferred_element_type=F32)
    rest = jnp.dot(inv_ref[:, 2 * size :], z_ref[at, :size], preferred_element_type=F32)
    return both + rest


def put_split(z_ref, at, rows, size, lanes, value):
    high = value.astype(BF16)
    z_ref[at, rows, lanes] = high
    low = pl.ds(rows.start + size, rows.size)
    z_ref[at, low, lanes] = (value - high.astype(F32)).astype(BF16)


def lane_parts(chans):
    return [slice(lo, min(lo + 128, chans)) for lo in range(0, chans, 128)]


def filter_kernel(taps_ref, tab_ref, out_ref, spec):
    size, block = tab_ref.shape[0], tab_ref.shape[0] // 2
    reach = taps_ref.shape[0] // block
    half = block // 2
    for j in range(reach):
        spec[j] = forward(tab_ref, taps_ref[j * block : (j + 1) * block])
    for e in range(reach + 1):
        for odd in range(2):
            sign = -1.0 if odd else 1.0
            cs = slice(odd * half, (odd + 1) * half)
            sn = slice(block + odd * half, block + (odd + 1) * half)
            if e == 0:
                real, imag = spec[0, cs], spec[0, sn]
            elif e == reach:
                real, imag = sign * spec[e - 1, sn], -sign * spec[e - 1, cs]
            else:
                real = spec[e, cs] + sign * spec[e - 1, sn]
                imag = spec[e, sn] - sign * spec[e - 1, cs]
            out_ref[e, cs] = real
            out_ref[e, sn] = imag


def pick_block(refs, choice, parity, user):
    if isinstance(choice, int):
        return refs[choice][user]
    even, odd = choice
    return jnp.where(parity == 0, refs[even][user], refs[odd][user])


def conv_kernel(choices, n_blocks, scal_ref, *refs):
    blocks = refs[:n_blocks]
    (grad_ref, gate_ref, gg_ref, e_ref, tab_ref, inv_ref) = refs[n_blocks : n_blocks + 6]
    gated_ref, ggate_ref, fg_ref = refs[n_blocks + 6 : n_blocks + 9]
    spec, gspec, z_ref = refs[n_blocks + 9 :]
    users, block, chans = grad_ref.shape
    size = 2 * block
    reach = len(choices) - 1
    half = block // 2
    parity = scal_ref[0]
    row = lax.broadcasted_iota(jnp.int32, (block, chans), 0)
    for u in range(users):
        gspec[u] = forward(tab_ref, grad_ref[u])
        for e in range(reach + 1):
            count = scal_ref[1 + e * users + u]
            value = pick_block(blocks, choices[e], parity, u)
            value = jnp.where(row < count, value.astype(F32), 0.0).astype(BF16)
            spec[e, u] = forward(tab_ref, value)

    step = 16
    for odd in range(2):
        sign = -1.0 if odd else 1.0

        @pl.loop(0, half // step)
        def _(t):
            base = pl.multiple_of(odd * half + t * step, step)
            cs, sn = pl.ds(base, step), pl.ds(block + base, step)
            for lanes in lane_parts(chans):
                g = [(gspec[u, cs, lanes], gspec[u, sn, lanes]) for u in range(users)]
                y = [None] * users
                before = None
                for e in range(reach + 1):
                    ec, es = e_ref[e, cs, lanes], e_ref[e, sn, lanes]
                    wc = ws = None
                    for u in range(users):
                        ac, as_ = spec[e, u, cs, lanes], spec[e, u, sn, lanes]
                        gc, gs = g[u]
                        yc, ys = ac * ec - as_ * es, ac * es + as_ * ec
                        y[u] = (yc, ys) if e == 0 else (y[u][0] + yc, y[u][1] + ys)
                        pc, ps = gc * ac + gs * as_, gs * ac - gc * as_
                        wc, ws = (pc, ps) if u == 0 else (wc + pc, ws + ps)
                    if before is not None:
                        at = users + e - 1
                        put_split(z_ref, at, cs, size, lanes, before[0] - sign * ws)
                        put_split(z_ref, at, sn, size, lanes, before[1] + sign * wc)
                    before = (wc, ws)
                for u in range(users):
                    put_split(z_ref, u, cs, size, lanes, y[u][0])
                    put_split(z_ref, u, sn, size, lanes, y[u][1])

    for u in range(users):
        conv = backward(inv_ref, z_ref, u, size)
        gate = gate_ref[u].astype(F32)
        sig = jax.nn.sigmoid(gate)
        live = (row < scal_ref[1 + u]).astype(F32)
        gated_ref[u] = (gate * sig * conv * live).astype(BF16)
        ggate_ref[u] = (gg_ref[u] * conv * sig * (1.0 + gate * (1.0 - sig))).astype(BF16)
    for j in range(reach):
        fg_ref[j] = backward(inv_ref, z_ref, users + j, size)


def input_kernel(choices, n_blocks, scal_ref, *refs):
    blocks = refs[:n_blocks]
    e_ref, tab_ref, inv_ref, out_ref, spec, z_ref = refs[n_blocks:]
    users, block, chans = blocks[0].shape
    size = 2 * block
    reach = len(choices) - 1
    parity = scal_ref[0]
    row = lax.broadcasted_iota(jnp.int32, (block, chans), 0)
    for u in range(users):
        for e in range(reach + 1):
            spec[e, u] = forward(tab_ref, pick_block(blocks, choices[e], parity, u))

    step = 16

    @pl.loop(0, block // step)
    def _(t):
        base = pl.multiple_of(t * step, step)
        cs, sn = pl.ds(base, step), pl.ds(block + base, step)
        for lanes in lane_parts(chans):
            z = [None] * users
            for e in range(reach + 1):
                ec, es = e_ref[e, cs, lanes], e_ref[e, sn, lanes]
                for u in range(users):
                    gc, gs = spec[e, u, cs, lanes], spec[e, u, sn, lanes]
                    zc, zs = gc * ec + gs * es, gs * ec - gc * es
                    z[u] = (zc, zs) if e == 0 else (z[u][0] + zc, z[u][1] + zs)
            for u in range(users):
                put_split(z_ref, u, cs, size, lanes, z[u][0])
                put_split(z_ref, u, sn, size, lanes, z[u][1])

    for u in range(users):
        value = backward(inv_ref, z_ref, u, size)
        out_ref[u] = jnp.where(row < scal_ref[1 + u], value, 0.0).astype(BF16)


def chan_tile(chans):
    return 256 if chans % 256 == 0 else chans


def whole(array):
    return pl.BlockSpec(array.shape, lambda c, *_: (0,) * array.ndim)


def by_chans(shape, tile):
    return pl.BlockSpec(
        shape[:-1] + (tile,), lambda c, *_: (0,) * (len(shape) - 1) + (c,)
    )


def cost(flops, size):
    return pl.CostEstimate(flops=flops, bytes_accessed=size, transcendentals=0)


def filter_spectra(filters, fwd):
    taps_len, chans = filters.shape
    size = fwd.shape[0]
    reach = taps_len // (size // 2)
    tile = chan_tile(chans)
    out = jax.ShapeDtypeStruct((reach + 1, size, chans), F32)
    return pl.pallas_call(
        filter_kernel,
        grid=(chans // tile,),
        in_specs=[by_chans(filters.shape, tile), whole(fwd)],
        out_specs=by_chans(out.shape, tile),
        out_shape=out,
        scratch_shapes=[pltpu.VMEM((reach, size, tile), F32)],
        cost_estimate=cost(2 * reach * size * size * chans, out.size * 4),
        name="filter_spectra",
    )(filters, fwd)


def conv_call(scal, choices, blocks, grad_conv, gate, grad_gated, spectra, fwd, inv):
    users, block, chans = grad_conv.shape
    size = 2 * block
    reach = len(choices) - 1
    tile = chan_tile(chans)
    outs = [
        jax.ShapeDtypeStruct(gate.shape, BF16),
        jax.ShapeDtypeStruct(gate.shape, BF16),
        jax.ShapeDtypeStruct((reach, block, chans), F32),
    ]
    moved = [*blocks, grad_conv, gate, grad_gated, spectra]
    grid_spec = pltpu.PrefetchScalarGridSpec(
        num_scalar_prefetch=1,
        grid=(chans // tile,),
        in_specs=[by_chans(a.shape, tile) for a in moved] + [whole(fwd), whole(inv)],
        out_specs=[by_chans(o.shape, tile) for o in outs],
        scratch_shapes=[
            pltpu.VMEM((reach + 1, users, size, tile), F32),
            pltpu.VMEM((users, size, tile), F32),
            pltpu.VMEM((users + reach, 2 * size, tile), BF16),
        ],
    )
    flops = 2 * chans * size * size * ((reach + 2) * users + 2 * (users + reach))
    return pl.pallas_call(
        functools.partial(conv_kernel, choices, len(blocks)),
        grid_spec=grid_spec,
        out_shape=outs,
        cost_estimate=cost(flops, sum(a.size * a.dtype.itemsize for a in moved)),
        name="conv",
    )(scal, *moved, fwd, inv)


def input_call(scal, choices, blocks, spectra, fwd, inv):
    users, block, chans = blocks[0].shape
    size = 2 * block
    reach = len(choices) - 1
    tile = chan_tile(chans)
    moved = [*blocks, spectra]
    out = jax.ShapeDtypeStruct(blocks[0].shape, BF16)
    grid_spec = pltpu.PrefetchScalarGridSpec(
        num_scalar_prefetch=1,
        grid=(chans // tile,),
        in_specs=[by_chans(a.shape, tile) for a in moved] + [whole(fwd), whole(inv)],
        out_specs=by_chans(out.shape, tile),
        scratch_shapes=[
            pltpu.VMEM((reach + 1, users, size, tile), F32),
            pltpu.VMEM((users, 2 * size, tile), BF16),
        ],
    )
    flops = 2 * chans * size * size * ((reach + 1) * users + 2 * users)
    return pl.pallas_call(
        functools.partial(input_kernel, choices, len(blocks)),
        grid_spec=grid_spec,
        out_shape=out,
        cost_estimate=cost(flops, sum(a.size * a.dtype.itemsize for a in moved)),
        name="grad_input",
    )(scal, *moved, fwd, inv)


def shifted(value, axis, by):
    count = lax.axis_size(axis)
    pairs = [(i, i + by) for i in range(count) if 0 <= i + by < count]
    return lax.ppermute(value, axis, pairs)


def swapped(value, axis, bit, only=None):
    pairs = [(i, i ^ bit) for i in range(lax.axis_size(axis))]
    if only is not None:
        pairs = [(i, j) for i, j in pairs if i % 2 == only]
    return lax.ppermute(value, axis, pairs)


def halo(value, reach, way):
    count = lax.axis_size("seq")
    if reach != 4 or count % 2:
        arrays = [value] + [shifted(value, "seq", way * k) for k in range(1, reach + 1)]
        return arrays, list(range(reach + 1))
    one = shifted(value, "seq", 2 * way)
    near = 0 if way == 1 else 1
    own_swap = swapped(value, "seq", 1, only=near)
    two = shifted(one, "seq", 2 * way)
    one_swap = swapped(one, "seq", 1)
    two_swap = swapped(two, "seq", 1, only=1 - near)
    arrays = [value, own_swap, one, one_swap, two, two_swap]
    if way == 1:
        return arrays, [0, (3, 1), 2, (5, 3), 4]
    return arrays, [0, (1, 3), 2, (3, 5), 4]


def is_power(n):
    return n & (n - 1) == 0


def sum_stages():
    dp, seq = lax.axis_size("dp"), lax.axis_size("seq")
    if not (is_power(dp) and is_power(seq)):
        return None
    stages = [("seq", 1)] if seq > 1 else []
    bit = 1
    while bit < dp:
        stages.append(("dp", bit))
        bit *= 2
    bit = 2
    while bit < seq:
        stages.append(("seq", bit))
        bit *= 2
    return stages


def sum_over(value, scale):
    stages = sum_stages()
    rows = value.shape[0]
    if stages is None or rows % (16 << len(stages)):
        return lax.psum(value, ("dp", "seq")) * scale
    sides = [(lax.axis_index(axis) // bit) % 2 for axis, bit in stages]
    for (axis, bit), side in zip(stages, sides):
        part = value.shape[0] // 2
        give = lax.dynamic_slice_in_dim(value, (1 - side) * part, part, 0).astype(BF16)
        keep = lax.dynamic_slice_in_dim(value, side * part, part, 0)
        value = keep + swapped(give, axis, bit).astype(F32)
    value = (value * scale).astype(BF16)
    for (axis, bit), side in reversed(list(zip(stages, sides))):
        other = swapped(value, axis, bit)
        low = jnp.where(side == 0, value, other)
        high = jnp.where(side == 0, other, value)
        value = jnp.concatenate([low, high], axis=0)
    return value.astype(F32)


def shards(events, gate_in, filters, proj, lengths, cotangent):
    users, block_len, chans = events.shape
    taps_len = filters.shape[0]
    reach = taps_len // block_len
    fwd_np, inv_np = tables(block_len)
    fwd, inv = jnp.asarray(fwd_np), jnp.asarray(inv_np)
    here = lax.axis_index("seq")
    first = here * block_len
    position = first + jnp.arange(block_len, dtype=jnp.int32)
    live = (position[None, :] < lengths[:, None]).astype(F32)[:, :, None]
    offsets = jnp.arange(reach + 1, dtype=jnp.int32) * block_len
    counts = lengths[None, :].astype(jnp.int32) - (first - offsets)[:, None]
    scal = jnp.concatenate(
        [(here % 2).astype(jnp.int32)[None], jnp.clip(counts, 0, block_len).reshape(-1)]
    )

    earlier, earlier_at = halo(events, reach, 1)
    spectra = filter_spectra(filters, fwd)

    n_tensor = lax.axis_size("tensor")
    cot_rows = cotangent.reshape(-1, chans)
    contract_last = (((1,), (1,)), ((), ()))
    contract_rows = (((0,), (0,)), ((), ()))
    if n_tensor == 2:
        mine = lax.axis_index("tensor")
        proj_own = lax.dynamic_slice_in_dim(proj, mine * chans, chans, 1)
        proj_other = lax.dynamic_slice_in_dim(proj, (1 - mine) * chans, chans, 1)
        cot_other = swapped(cot_rows, "tensor", 1)
        grad_acc = lax.dot_general(
            cot_rows, proj_own, contract_last, preferred_element_type=F32
        ) + lax.dot_general(cot_other, proj_other, contract_last, preferred_element_type=F32)
    else:
        cot_all = lax.all_gather(cot_rows, "tensor", axis=1, tiled=True)
        grad_acc = lax.dot_general(cot_all, proj, contract_last, preferred_element_type=F32)

    gate_f = gate_in.astype(F32)
    silu_g = gate_f * jax.nn.sigmoid(gate_f)
    grad_gated = grad_acc.reshape(users, block_len, chans) * live
    grad_conv = (grad_gated * silu_g).astype(BF16)
    later, later_at = halo(grad_conv, reach, -1)

    gated, grad_gate, filter_parts = conv_call(
        scal, earlier_at, earlier, grad_conv, gate_in, grad_gated, spectra, fwd, inv
    )
    rows = users * lax.axis_size("dp") * block_len * lax.axis_size("seq")
    scale = 1.0 / math.sqrt(rows)
    grad_filters = sum_over(filter_parts.reshape(taps_len, chans), scale)
    gated_rows = gated.reshape(-1, chans)
    if n_tensor == 2:
        part_other = jnp.dot(gated_rows, proj_other, preferred_element_type=F32)
        arrived = swapped(part_other.astype(BF16), "tensor", 1)
        out_rows = jnp.dot(gated_rows, proj_own, preferred_element_type=F32) + arrived.astype(F32)
        outer_own = lax.dot_general(gated_rows, cot_rows, contract_rows, preferred_element_type=F32)
        outer_other = lax.dot_general(
            gated_rows, cot_other, contract_rows, preferred_element_type=F32
        )
        sum_own, sum_other = sum_over(outer_own, scale), sum_over(outer_other, scale)
        grad_proj = jnp.concatenate(
            [
                jnp.where(mine == 0, sum_own, sum_other),
                jnp.where(mine == 0, sum_other, sum_own),
            ],
            axis=1,
        )
    else:
        partial_out = jnp.dot(gated_rows, proj, preferred_element_type=F32)
        out_rows = lax.psum_scatter(partial_out, "tensor", scatter_dimension=1, tiled=True)
        outer = lax.dot_general(gated_rows, cot_all, contract_rows, preferred_element_type=F32)
        grad_proj = sum_over(outer, scale)
    mixed = out_rows.astype(BF16).reshape(users, block_len, chans)
    grad_input = input_call(scal, later_at, later, spectra, fwd, inv)
    return (mixed, grad_input, grad_gate, grad_filters, grad_proj)


def solution(mesh):
    in_specs = (
        P("dp", "seq", "tensor"),
        P("dp", "seq", "tensor"),
        P(None, "tensor"),
        P("tensor", None),
        P("dp"),
        P("dp", "seq", "tensor"),
    )
    out_specs = (
        P("dp", "seq", "tensor"),
        P("dp", "seq", "tensor"),
        P("dp", "seq", "tensor"),
        P(None, "tensor"),
        P("tensor", None),
    )
    return jax.shard_map(shards, mesh=mesh, in_specs=in_specs, out_specs=out_specs, check_vma=False)
```

time: 1050 us -> 181 us (0.17); the launches traced: 1040 us -> 180 us
  matrix products: 622 us -> 13 us
  waiting for transfers between devices: 252 us -> 56.4 us
  local copies, waits for them, and re-layouts: 101 us -> 4.28 us
  Pallas kernels: 0 us -> 40.9 us
  starting transfers between devices: 20.9 us -> 50.9 us
  other arithmetic: 27.1 us -> 13.2 us
  between operations: 14.4 us -> 1.33 us
    conv_general_dilated x3 -> x0, matrix products: 613 us -> none  [depthwise(): lax.conv_general_dilated(lhs, kernel[:, None, :], (1,), 'VALID', dimensio...]
    psum x1 -> x0, waiting for transfers between devices: 197 us -> none  [shards(): filter_sum, proj_sum = lax.psum((filter_local, outer), ('dp', 'seq'))]
    rev x2 -> x0, local copies, waits for them, and re-layouts: 47.7 us -> none  [the longest x1 24.7 us: filter_grad(): return jnp.sum(result.reshape(-1, users, chans), axis=1)[::-1]]
    pallas_call x0 -> x3, Pallas kernels: none -> 40.9 us  [the longest x1 21.4 us: conv_call(): pl.pallas_call(functools.partial(conv_kernel, choices, len(blocks)), grid...]
    reduce_scatter x1 -> x0, waiting for transfers between devices: 39.1 us -> none  [shards(): lax.psum_scatter(partial_out, 'tensor', scatter_dimension=1, tiled=True)]
    ppermute x0 -> x32, waiting for transfers between devices: none -> 37.3 us  [swapped(): return lax.ppermute(value, axis, pairs)]
    ppermute x0 -> x32, starting transfers between devices: none -> 37 us  [swapped(): return lax.ppermute(value, axis, pairs)]
    reshape x2 -> x0, local copies, waits for them, and re-layouts: 24.9 us -> none  [the longest x1 16.7 us: filter_grad(): lhs = jnp.transpose(window, (1, 0, 2)).reshape(1, width, users * chans)]
  transfers between devices with their start and end apart: 11 -> 36, of which waited for: 4 -> 12; matrix products, arithmetic and copies ran while one was open for 52% -> 15% of each run, Pallas kernels for 0% -> 23%
where the time goes in v1:
time: 181 us; the launch traced here: 180 us
  waiting for transfers between devices  56.4 us (31%)
  starting transfers between devices  50.9 us (28%)
  Pallas kernels  40.9 us (23%)
  other arithmetic  13.2 us (7%)
  matrix products  13 us (7%)
  local copies, waits for them, and re-layouts  4.28 us (2%)
    ppermute x32, waiting for transfers between devices, swapped(): return lax.ppermute(value, axis, pairs)  37.3 us
    ppermute x32, starting transfers between devices, swapped(): return lax.ppermute(value, axis, pairs)  37 us
    pallas_call x1, Pallas kernels, conv_call(): pl.pallas_call(functools.partial(conv_kernel, choices, len(blocks)), grid...  21.4 us
    ppermute x4, waiting for transfers between devices, shifted(): return lax.ppermute(value, axis, pairs)  19.1 us
    ppermute x4, starting transfers between devices, shifted(): return lax.ppermute(value, axis, pairs)  13.9 us
    pallas_call x1, Pallas kernels, input_call(): pl.pallas_call(functools.partial(input_kernel, choices, len(blocks)), gri...  13.6 us
    pallas_call x1, Pallas kernels, filter_spectra(): pl.pallas_call(filter_kernel, grid=(chans // tile,), in_specs=[by_chans(f...  5.85 us
    add x9, other arithmetic, sum_over(): value = keep + swapped(give, axis, bit).astype(F32)  3.67 us
  transfers between devices with their start and end apart: 36, of which 12 were waited for; matrix products, arithmetic and copies ran while one was open for 15% of the time, Pallas kernels for 23%

profile of v1, /device:TPU:0, one launch (start us, length us, event | category | flops | bytes accessed | tf_op | source)
XLA Modules:
  0.0 180.0 jit_solution(8640445122050646869)
XLA Ops:
  0.6 6.0 %collective-permute-start.1 = (bf16[2,256,768]{2,1,0:T(8,128)(2,1)}, bf16[2,256,768]{2,1,0:T(8,128)(2,1)}, u32[]{:S(2)}, u32[]{:S(2)}) collective-permute-start(bf16[2,256,768]{2,1,0:T(8,128)(2,1)} %refs_0_.1), channel_id=1, source_target_pairs={{0,4},{2,6},{4,8},{6,10},{8,12},{10,14},{1,5},{3,7},{5,9},{7,11},{... | collective-permute-start | bytes 2359304 | tf_op jit(solution)/shard_map/ppermute | solution.py:279
  6.6 1.5 collective-permute-start.5
  8.2 3.1 %fusion.8 = f32[768,512]{0,1:T(8,128)} fusion(bf16[512,768]{1,0:T(8,128)(2,1)} %bitcast.25, bf16[768,1536]{1,0:T(8,128)(2,1)S(1)} %copy-done, s32[]{:T(128)S(6)} %select_n.257), kind=kOutput, calls=%fused_computation.26 | convolution fusion | flops 603979776 | bytes 3538948 | tf_op jit(solution)/shard_map/dot_general | solution.py:374
  11.3 11.6 %collective-permute-done.1.refs_2_ = bf16[2,256,768]{2,1,0:T(8,128)(2,1)} collective-permute-done((bf16[2,256,768]{2,1,0:T(8,128)(2,1)}, bf16[2,256,768]{2,1,0:T(8,128)(2,1)}, u32[]{:S(2)}, u32[]{:S(2)}) %collective-permute-start.1) | collective-permute-done | bytes 786464 | tf_op jit(solution)/shard_map/ppermute | solution.py:279
  22.8 5.3 %collective-permute-start.3 = (bf16[2,256,768]{2,1,0:T(8,128)(2,1)}, bf16[2,256,768]{2,1,0:T(8,128)(2,1)}, u32[]{:S(2)}, u32[]{:S(2)}) collective-permute-start(bf16[2,256,768]{2,1,0:T(8,128)(2,1)} %collective-permute-done.1.refs_2_), channel_id=1, source_target_pairs={{0,4},{2,6},{4,8},{6,10},{8,12},{10,14},{1,5},{3,7},{5,9},{7,11},{... | collective-permute-start | bytes 2359304 | tf_op jit(solution)/shard_map/ppermute | solution.py:279
  28.3 2.3 %convolution_add_fusion = f32[768,512]{0,1:T(8,128)S(1)} fusion(f32[768,512]{0,1:T(8,128)} %fusion.8, bf16[512,768]{1,0:T(8,128)(2,1)S(1)} %collective-permute-done.5, bf16[768,1536]{1,0:T(8,128)(2,1)S(1)} %copy-done, s32[]{:T(128)S(6)} %select_n.258), kind=kOutput, calls=%fused_computation.15 | convolution fusion | flops 604372992 | bytes 5111812 | tf_op jit(solution)/shard_map/dot_general | solution.py:376
  30.6 1.9 %fusion.4 = (bf16[2,256,768]{2,1,0:T(8,128)(2,1)}, f32[2,256,768]{2,1,0:T(8,128)}) fusion(bf16[2,256,768]{2,1,0:T(8,128)(2,1)S(1)} %copy-done.7, f32[2,256,768]{2,1,0:T(8,128)S(1)} %bitcast.18, f32[2,256]{1,0:T(2,128)S(1)} %compare_convert_fusion), kind=kLoop, calls=%fused_computation.14 | loop fusion | flops 3145728 | bytes 4720640 | tf_op jit(solution)/shard_map/convert_element_type | solution.py:384
  32.5 1.3 collective-permute-start.8
  33.8 2.2 %collective-permute-start = (bf16[2,256,768]{2,1,0:T(8,128)(2,1)}, bf16[2,256,768]{2,1,0:T(8,128)(2,1)}, u32[]{:S(2)}, u32[]{:S(2)}) collective-permute-start(bf16[2,256,768]{2,1,0:T(8,128)(2,1)} %refs_0_.1), channel_id=1, source_target_pairs={{0,2},{4,6},{8,10},{12,14},{1,3},{5,7},{9,11},{13,15},{16,18},{20,... | collective-permute-start | bytes 2359304 | tf_op jit(solution)/shard_map/ppermute | solution.py:286
  36.0 7.5 %collective-permute-done.3.refs_4_ = bf16[2,256,768]{2,1,0:T(8,128)(2,1)} collective-permute-done((bf16[2,256,768]{2,1,0:T(8,128)(2,1)}, bf16[2,256,768]{2,1,0:T(8,128)(2,1)}, u32[]{:S(2)}, u32[]{:S(2)}) %collective-permute-start.3) | collective-permute-done | bytes 786464 | tf_op jit(solution)/shard_map/ppermute | solution.py:279
  43.5 1.3 collective-permute-start.4
  45.8 5.8 %filter_spectra.1.refs_9_.refs_6_ = f32[5,512,768]{2,1,0:T(8,128)} custom-call(bf16[1024,768]{1,0:T(8,128)(2,1)} %taps_ref.1, bf16[512,512]{1,0:T(8,128)(2,1)} %constant.143.clone.tab_ref.refs_10_.refs_7_), custom_call_target="tpu_custom_call" | custom-call | flops 1610612736 | bytes 7864320 | tf_op jit(solution)/shard_map/filter_spectra/pallas_call | solution.py:205
  51.6 1.3 collective-permute-start.7
  52.9 1.3 collective-permute-start.10
  54.2 21.4 %conv.1 = (bf16[2,256,768]{2,1,0:T(8,128)(2,1)}, bf16[2,256,768]{2,1,0:T(8,128)(2,1)}, f32[4,256,768]{2,1,0:T(8,128)}) custom-call(s32[11]{0:T(128)} %pad_add_fusion.scal_ref, bf16[2,256,768]{2,1,0:T(8,128)(2,1)} %refs_0_.1, bf16[2,256,768]{2,1,0:T(8,128)(2,1)} %collective-permute-done.refs_1_, bf16[2,256,768]{2,1,0:T(8,128)(2,1)} %collective-permute-done.1.refs_2_, ...), custom_call_target="tpu_custom_call" | custom-call | flops 9663676416 | bytes 15728640 | tf_op jit(solution)/shard_map/conv/pallas_call | solution.py:240
  75.6 2.1 %fusion.14 = f32[768,768]{1,0:T(8,128)S(1)} fusion(bf16[512,768]{1,0:T(8,128)(2,1)} %bitcast.19, bf16[512,768]{1,0:T(8,128)(2,1)S(1)} %collective-permute-done.5), kind=kOutput, calls=%fused_computation.89 | convolution fusion | flops 603979776 | bytes 3932160 | tf_op jit(solution)/shard_map/dot_general | solution.py:399
  77.8 2.8 %collective-permute-start.28 = (bf16[384,768]{1,0:T(8,128)(2,1)S(1)}, bf16[384,768]{1,0:T(8,128)(2,1)S(1)}, u32[]{:S(2)}, u32[]{:S(2)}) collective-permute-start(bf16[384,768]{1,0:T(8,128)(2,1)S(1)} %dynamic-slice_convert_fusion.1), channel_id=1, source_target_pairs={{0,2},{2,0},{4,6},{6,4},{8,10},{10,8},{12,14},{14,12},{1,3},{3,1},... | collective-permute-start | bytes 1769480 | tf_op jit(solution)/shard_map/ppermute | solution.py:286
  81.5 1.0 collective-permute-start.12
  82.7 1.7 convolution_convert_fusion
  85.8 1.5 collective-permute-start.6
  87.3 2.5 %collective-permute-start.11 = (bf16[2,256,768]{2,1,0:T(8,128)(2,1)}, bf16[2,256,768]{2,1,0:T(8,128)(2,1)}, u32[]{:S(2)}, u32[]{:S(2)}) collective-permute-start(bf16[2,256,768]{2,1,0:T(8,128)(2,1)} %collective-permute-done.10.refs_4_), channel_id=1, source_target_pairs={{0,2},{4,6},{8,10},{12,14},{1,3},{5,7},{9,11},{13,15},{16,18},{20,... | collective-permute-start | bytes 2359304 | tf_op jit(solution)/shard_map/ppermute | solution.py:286
  90.0 0.8 dynamic-slice_convert_fusion.5
  91.1 1.5 collective-permute-start.29
  92.7 1.1 copy-done.1
  95.2 1.5 collective-permute-start.13
  96.7 13.6 %grad_input.1 = bf16[2,256,768]{2,1,0:T(8,128)(2,1)} custom-call(s32[11]{0:T(128)} %pad_add_fusion.scal_ref, bf16[2,256,768]{2,1,0:T(8,128)(2,1)} %get-tuple-element.11.refs_6_.refs_0_, bf16[2,256,768]{2,1,0:T(8,128)(2,1)} %collective-permute-done.7.refs_1_, bf16[2,256,768]{2,1,0:T(8,128)(2,1)} %collective-permute-done.8.refs_2_, ...), custom_call_target="tpu_custom_call" | custom-call | flops 5637144576 | bytes 12582912 | tf_op jit(solution)/shard_map/grad_input/pallas_call | solution.py:267
  110.3 3.0 %add_convert_fusion = bf16[512,768]{1,0:T(8,128)(2,1)} fusion(bf16[512,768]{1,0:T(8,128)(2,1)} %collective-permute-done.6, bf16[512,768]{1,0:T(8,128)(2,1)} %bitcast.20, bf16[768,1536]{1,0:T(8,128)(2,1)S(1)} %copy-done, s32[]{:T(128)S(6)} %select_n.257), kind=kOutput, calls=%fused_computation.13 | convolution fusion | flops 605159424 | bytes 3538948 | tf_op jit(solution)/shard_map/dot_general | solution.py:397
  113.4 1.1 convert_add_fusion.4
  114.5 3.2 %collective-permute-start.30 = (bf16[96,768]{1,0:T(8,128)(2,1)S(1)}, bf16[96,768]{1,0:T(8,128)(2,1)S(1)}, u32[]{:S(2)}, u32[]{:S(2)}) collective-permute-start(bf16[96,768]{1,0:T(8,128)(2,1)S(1)} %dynamic-slice_convert_fusion.7), channel_id=1, source_target_pairs={{0,4},{2,6},{4,0},{6,2},{8,12},{10,14},{12,8},{14,10},{1,5},{3,7},... | collective-permute-start | bytes 442376 | tf_op jit(solution)/shard_map/ppermute | solution.py:286
  117.7 1.0 convert_add_fusion.5
  119.0 3.2 %collective-permute-done.30 = bf16[96,768]{1,0:T(8,128)(2,1)S(1)} collective-permute-done((bf16[96,768]{1,0:T(8,128)(2,1)S(1)}, bf16[96,768]{1,0:T(8,128)(2,1)S(1)}, u32[]{:S(2)}, u32[]{:S(2)}) %collective-permute-start.30) | collective-permute-done | bytes 147488 | tf_op jit(solution)/shard_map/ppermute | solution.py:286
  122.2 3.9 %collective-permute-start.31 = (bf16[48,768]{1,0:T(8,128)(2,1)S(1)}, bf16[48,768]{1,0:T(8,128)(2,1)S(1)}, u32[]{:S(2)}, u32[]{:S(2)}) collective-permute-start(bf16[48,768]{1,0:T(8,128)(2,1)S(1)} %dynamic-slice_convert_fusion.10), channel_id=1, source_target_pairs={{0,8},{2,10},{4,12},{6,14},{8,0},{10,2},{12,4},{14,6},{1,9},{3,11}... | collective-permute-start | bytes 221192 | tf_op jit(solution)/shard_map/ppermute | solution.py:286
  126.2 2.9 %collective-permute-start.23 = (bf16[48,768]{1,0:T(8,128)(2,1)S(1)}, bf16[48,768]{1,0:T(8,128)(2,1)S(1)}, u32[]{:S(2)}, u32[]{:S(2)}) collective-permute-start(bf16[48,768]{1,0:T(8,128)(2,1)S(1)} %dynamic-slice_convert_fusion.11), channel_id=1, source_target_pairs={{0,8},{2,10},{4,12},{6,14},{8,0},{10,2},{12,4},{14,6},{1,9},{3,11}... | collective-permute-start | bytes 221192 | tf_op jit(solution)/shard_map/ppermute | solution.py:286
  129.0 3.5 %collective-permute-done.31 = bf16[48,768]{1,0:T(8,128)(2,1)S(1)} collective-permute-done((bf16[48,768]{1,0:T(8,128)(2,1)S(1)}, bf16[48,768]{1,0:T(8,128)(2,1)S(1)}, u32[]{:S(2)}, u32[]{:S(2)}) %collective-permute-start.31) | collective-permute-done | bytes 73760 | tf_op jit(solution)/shard_map/ppermute | solution.py:286
  132.7 1.5 collective-permute-done.23
  134.2 1.4 collective-permute-start.24
  135.7 1.1 convert_add_fusion.3
  136.8 2.3 %collective-permute-start.14 = (bf16[128,768]{1,0:T(8,128)(2,1)S(1)}, bf16[128,768]{1,0:T(8,128)(2,1)S(1)}, u32[]{:S(2)}, u32[]{:S(2)}) collective-permute-start(bf16[128,768]{1,0:T(8,128)(2,1)S(1)} %dynamic-slice_convert_fusion.6), channel_id=1, source_target_pairs={{0,4},{2,6},{4,0},{6,2},{8,12},{10,14},{12,8},{14,10},{1,5},{3,7},... | collective-permute-start | bytes 589832 | tf_op jit(solution)/shard_map/ppermute | solution.py:286
  139.3 0.9 collective-permute-done.24
  140.2 1.1 collective-permute-start.25
  141.4 4.7 %collective-permute-done.33 = bf16[96,768]{1,0:T(8,128)(2,1)S(1)} collective-permute-done((bf16[96,768]{1,0:T(8,128)(2,1)S(1)}, bf16[96,768]{1,0:T(8,128)(2,1)S(1)}, u32[]{:S(2)}, u32[]{:S(2)}) %collective-permute-start.33) | collective-permute-done | bytes 147488 | tf_op jit(solution)/shard_map/ppermute | solution.py:286
  147.7 5.7 %collective-permute-done.15 = bf16[64,768]{1,0:T(8,128)(2,1)S(1)} collective-permute-done((bf16[64,768]{1,0:T(8,128)(2,1)S(1)}, bf16[64,768]{1,0:T(8,128)(2,1)S(1)}, u32[]{:S(2)}, u32[]{:S(2)}) %collective-permute-start.15) | collective-permute-done | bytes 98336 | tf_op jit(solution)/shard_map/ppermute | solution.py:286
  153.5 1.3 collective-permute-start.26
  154.8 5.2 %collective-permute-done.16 = bf16[64,768]{1,0:T(8,128)(2,1)S(1)} collective-permute-done((bf16[64,768]{1,0:T(8,128)(2,1)S(1)}, bf16[64,768]{1,0:T(8,128)(2,1)S(1)}, u32[]{:S(2)}, u32[]{:S(2)}) %collective-permute-start.16) | collective-permute-done | bytes 98336 | tf_op jit(solution)/shard_map/ppermute | solution.py:286
  160.3 5.5 %collective-permute-done.17 = bf16[128,768]{1,0:T(8,128)(2,1)S(1)} collective-permute-done((bf16[128,768]{1,0:T(8,128)(2,1)S(1)}, bf16[128,768]{1,0:T(8,128)(2,1)S(1)}, u32[]{:S(2)}, u32[]{:S(2)}) %collective-permute-start.17) | collective-permute-done | bytes 196640 | tf_op jit(solution)/shard_map/ppermute | solution.py:286
  166.8 6.9 %collective-permute-done.18 = bf16[256,768]{1,0:T(8,128)(2,1)S(1)} collective-permute-done((bf16[256,768]{1,0:T(8,128)(2,1)S(1)}, bf16[256,768]{1,0:T(8,128)(2,1)S(1)}, u32[]{:S(2)}, u32[]{:S(2)}) %collective-permute-start.18) | collective-permute-done | bytes 393248 | tf_op jit(solution)/shard_map/ppermute | solution.py:286
  174.9 2.9 %pad_maximum_fusion = f32[768,1536]{1,0:T(8,128)} fusion(f32[768,768]{1,0:T(8,128)S(1)} %get-tuple-element.14, f32[768,768]{1,0:T(8,128)S(1)} %get-tuple-element.13), kind=kLoop, calls=%fused_computation | loop fusion | flops 1179648 | bytes 9437184 | tf_op jit(solution)/shard_map/concatenate | solution.py:403
  178.1 1.9 %maximum_convert_fusion = f32[1024,768]{1,0:T(8,128)} fusion(bf16[512,768]{1,0:T(8,128)(2,1)S(1)} %get-tuple-element.16, bf16[512,768]{1,0:T(8,128)(2,1)S(1)} %get-tuple-element.15), kind=kLoop, calls=%fused_computation.10 | loop fusion | flops 3145728 | bytes 4718592 | tf_op jit(solution)/shard_map/convert_element_type | solution.py:343
  (108 shorter events, 10.3 us)
Async XLA Ops:
  0.6 7.5 %copy-start = (bf16[768,1536]{1,0:T(8,128)(2,1)S(1)}, bf16[768,1536]{1,0:T(8,128)(2,1)}, u32[]{:S(2)}) copy-start(bf16[768,1536]{1,0:T(8,128)(2,1)} %param.11) | copy-start | bytes 7077892
  0.6 22.2 %collective-permute-start.1 = (bf16[2,256,768]{2,1,0:T(8,128)(2,1)}, bf16[2,256,768]{2,1,0:T(8,128)(2,1)}, u32[]{:S(2)}, u32[]{:S(2)}) collective-permute-start(bf16[2,256,768]{2,1,0:T(8,128)(2,1)} %refs_0_.1), channel_id=1, source_target_pairs={{0,4},{2,6},{4,8},{6,10},{8,12},{10,14},{1,5},{3,7},{5,9},{7,11},{... | collective-permute-start | bytes 2359304 | tf_op jit(solution)/shard_map/ppermute | solution.py:279
  6.6 21.6 %collective-permute-start.5 = (bf16[512,768]{1,0:T(8,128)(2,1)}, bf16[512,768]{1,0:T(8,128)(2,1)S(1)}, u32[]{:S(2)}, u32[]{:S(2)}) collective-permute-start(bf16[512,768]{1,0:T(8,128)(2,1)} %bitcast.24), channel_id=1, source_target_pairs={{0,1},{1,0},{2,3},{3,2},{4,5},{5,4},{6,7},{7,6},{8,9},{9,8},{10,11... | collective-permute-start | bytes 2359304 | tf_op jit(solution)/shard_map/ppermute | solution.py:286
  8.2 20.0 %copy-start.8 = (s32[2]{0:T(128)S(1)}, s32[2]{0:T(128)}, u32[]{:S(2)}) copy-start(s32[2]{0:T(128)} %param.12) | copy-start | bytes 28
  22.8 20.6 %collective-permute-start.3 = (bf16[2,256,768]{2,1,0:T(8,128)(2,1)}, bf16[2,256,768]{2,1,0:T(8,128)(2,1)}, u32[]{:S(2)}, u32[]{:S(2)}) collective-permute-start(bf16[2,256,768]{2,1,0:T(8,128)(2,1)} %collective-permute-done.1.refs_2_), channel_id=1, source_target_pairs={{0,4},{2,6},{4,8},{6,10},{8,12},{10,14},{1,5},{3,7},{5,9},{7,11},{... | collective-permute-start | bytes 2359304 | tf_op jit(solution)/shard_map/ppermute | solution.py:279
  28.2 2.3 %copy-start.7 = (bf16[2,256,768]{2,1,0:T(8,128)(2,1)S(1)}, bf16[2,256,768]{2,1,0:T(8,128)(2,1)}, u32[]{:S(2)}) copy-start(bf16[2,256,768]{2,1,0:T(8,128)(2,1)} %refs_7_.2) | copy-start | bytes 2359300
  32.5 20.4 %collective-permute-start.8 = (bf16[2,256,768]{2,1,0:T(8,128)(2,1)}, bf16[2,256,768]{2,1,0:T(8,128)(2,1)}, u32[]{:S(2)}, u32[]{:S(2)}) collective-permute-start(bf16[2,256,768]{2,1,0:T(8,128)(2,1)} %get-tuple-element.11.refs_6_.refs_0_), channel_id=1, source_target_pairs={{4,0},{6,2},{8,4},{10,6},{12,8},{14,10},{5,1},{7,3},{9,5},{11,7},{... | collective-permute-start | bytes 2359304 | tf_op jit(solution)/shard_map/ppermute | solution.py:279
  33.8 20.4 %collective-permute-start = (bf16[2,256,768]{2,1,0:T(8,128)(2,1)}, bf16[2,256,768]{2,1,0:T(8,128)(2,1)}, u32[]{:S(2)}, u32[]{:S(2)}) collective-permute-start(bf16[2,256,768]{2,1,0:T(8,128)(2,1)} %refs_0_.1), channel_id=1, source_target_pairs={{0,2},{4,6},{8,10},{12,14},{1,3},{5,7},{9,11},{13,15},{16,18},{20,... | collective-permute-start | bytes 2359304 | tf_op jit(solution)/shard_map/ppermute | solution.py:286
  36.0 18.3 %collective-permute-start.2 = (bf16[2,256,768]{2,1,0:T(8,128)(2,1)}, bf16[2,256,768]{2,1,0:T(8,128)(2,1)}, u32[]{:S(2)}, u32[]{:S(2)}) collective-permute-start(bf16[2,256,768]{2,1,0:T(8,128)(2,1)} %collective-permute-done.1.refs_2_), channel_id=1, source_target_pairs={{0,2},{2,0},{4,6},{6,4},{8,10},{10,8},{12,14},{14,12},{1,3},{3,1},... | collective-permute-start | bytes 2359304 | tf_op jit(solution)/shard_map/ppermute | solution.py:286
  43.5 10.8 %collective-permute-start.4 = (bf16[2,256,768]{2,1,0:T(8,128)(2,1)}, bf16[2,256,768]{2,1,0:T(8,128)(2,1)}, u32[]{:S(2)}, u32[]{:S(2)}) collective-permute-start(bf16[2,256,768]{2,1,0:T(8,128)(2,1)} %collective-permute-done.3.refs_4_), channel_id=1, source_target_pairs={{2,0},{6,4},{10,8},{14,12},{3,1},{7,5},{11,9},{15,13},{18,16},{22,... | collective-permute-start | bytes 2359304 | tf_op jit(solution)/shard_map/ppermute | solution.py:286
  51.6 43.1 %collective-permute-start.7 = (bf16[2,256,768]{2,1,0:T(8,128)(2,1)}, bf16[2,256,768]{2,1,0:T(8,128)(2,1)}, u32[]{:S(2)}, u32[]{:S(2)}) collective-permute-start(bf16[2,256,768]{2,1,0:T(8,128)(2,1)} %get-tuple-element.11.refs_6_.refs_0_), channel_id=1, source_target_pairs={{2,0},{6,4},{10,8},{14,12},{3,1},{7,5},{11,9},{15,13},{18,16},{22,... | collective-permute-start | bytes 2359304 | tf_op jit(solution)/shard_map/ppermute | solution.py:286
  52.9 32.9 %collective-permute-start.10 = (bf16[2,256,768]{2,1,0:T(8,128)(2,1)}, bf16[2,256,768]{2,1,0:T(8,128)(2,1)}, u32[]{:S(2)}, u32[]{:S(2)}) collective-permute-start(bf16[2,256,768]{2,1,0:T(8,128)(2,1)} %collective-permute-done.8.refs_2_), channel_id=1, source_target_pairs={{4,0},{6,2},{8,4},{10,6},{12,8},{14,10},{5,1},{7,3},{9,5},{11,7},{... | collective-permute-start | bytes 2359304 | tf_op jit(solution)/shard_map/ppermute | solution.py:279
  75.6 5.0 %copy-start.5 = (bf16[2,256,768]{2,1,0:T(8,128)(2,1)S(1)}, bf16[2,256,768]{2,1,0:T(8,128)(2,1)}, u32[]{:S(2)}) copy-start(bf16[2,256,768]{2,1,0:T(8,128)(2,1)} %get-tuple-element.8) | copy-start | bytes 2359300
  75.6 5.0 %copy-start.9 = (bf16[2,256,768]{2,1,0:T(8,128)(2,1)S(1)}, bf16[2,256,768]{2,1,0:T(8,128)(2,1)}, u32[]{:S(2)}) copy-start(bf16[2,256,768]{2,1,0:T(8,128)(2,1)} %param.13) | copy-start | bytes 2359300
  77.8 3.6 %copy-start.6 = (f32[4,256,768]{2,1,0:T(8,128)S(1)}, f32[4,256,768]{2,1,0:T(8,128)}, u32[]{:S(2)}) copy-start(f32[4,256,768]{2,1,0:T(8,128)} %get-tuple-element.10) | copy-start | bytes 9437188
  77.8 6.6 %collective-permute-start.28 = (bf16[384,768]{1,0:T(8,128)(2,1)S(1)}, bf16[384,768]{1,0:T(8,128)(2,1)S(1)}, u32[]{:S(2)}, u32[]{:S(2)}) collective-permute-start(bf16[384,768]{1,0:T(8,128)(2,1)S(1)} %dynamic-slice_convert_fusion.1), channel_id=1, source_target_pairs={{0,2},{2,0},{4,6},{6,4},{8,10},{10,8},{12,14},{14,12},{1,3},{3,1},... | collective-permute-start | bytes 1769480 | tf_op jit(solution)/shard_map/ppermute | solution.py:286
  81.5 9.3 %collective-permute-start.12 = (bf16[512,768]{1,0:T(8,128)(2,1)S(1)}, bf16[512,768]{1,0:T(8,128)(2,1)S(1)}, u32[]{:S(2)}, u32[]{:S(2)}) collective-permute-start(bf16[512,768]{1,0:T(8,128)(2,1)S(1)} %dynamic-slice_convert_fusion), channel_id=1, source_target_pairs={{0,2},{2,0},{4,6},{6,4},{8,10},{10,8},{12,14},{14,12},{1,3},{3,1},... | collective-permute-start | bytes 2359304 | tf_op jit(solution)/shard_map/ppermute | solution.py:286
  82.6 4.7 %collective-permute-start.20 = (bf16[384,768]{1,0:T(8,128)(2,1)S(1)}, bf16[384,768]{1,0:T(8,128)(2,1)S(1)}, u32[]{:S(2)}, u32[]{:S(2)}) collective-permute-start(bf16[384,768]{1,0:T(8,128)(2,1)S(1)} %dynamic-slice_convert_fusion.2), channel_id=1, source_target_pairs={{0,2},{2,0},{4,6},{6,4},{8,10},{10,8},{12,14},{14,12},{1,3},{3,1},... | collective-permute-start | bytes 1769480 | tf_op jit(solution)/shard_map/ppermute | solution.py:286
  84.4 10.8 %collective-permute-start.9 = (bf16[2,256,768]{2,1,0:T(8,128)(2,1)}, bf16[2,256,768]{2,1,0:T(8,128)(2,1)}, u32[]{:S(2)}, u32[]{:S(2)}) collective-permute-start(bf16[2,256,768]{2,1,0:T(8,128)(2,1)} %collective-permute-done.8.refs_2_), channel_id=1, source_target_pairs={{0,2},{2,0},{4,6},{6,4},{8,10},{10,8},{12,14},{14,12},{1,3},{3,1},... | collective-permute-start | bytes 2359304 | tf_op jit(solution)/shard_map/ppermute | solution.py:286
  85.8 24.5 %collective-permute-start.6 = (bf16[512,768]{1,0:T(8,128)(2,1)}, bf16[512,768]{1,0:T(8,128)(2,1)}, u32[]{:S(2)}, u32[]{:S(2)}) collective-permute-start(bf16[512,768]{1,0:T(8,128)(2,1)} %convolution_convert_fusion), channel_id=1, source_target_pairs={{0,1},{1,0},{2,3},{3,2},{4,5},{5,4},{6,7},{7,6},{8,9},{9,8},{10,11... | collective-permute-start | bytes 2359304 | tf_op jit(solution)/shard_map/ppermute | solution.py:286
  87.3 9.4 %collective-permute-start.11 = (bf16[2,256,768]{2,1,0:T(8,128)(2,1)}, bf16[2,256,768]{2,1,0:T(8,128)(2,1)}, u32[]{:S(2)}, u32[]{:S(2)}) collective-permute-start(bf16[2,256,768]{2,1,0:T(8,128)(2,1)} %collective-permute-done.10.refs_4_), channel_id=1, source_target_pairs={{0,2},{4,6},{8,10},{12,14},{1,3},{5,7},{9,11},{13,15},{16,18},{20,... | collective-permute-start | bytes 2359304 | tf_op jit(solution)/shard_map/ppermute | solution.py:286
  90.0 1.1 copy-start.3
  91.1 22.3 %collective-permute-start.29 = (bf16[192,768]{1,0:T(8,128)(2,1)}, bf16[192,768]{1,0:T(8,128)(2,1)}, u32[]{:S(2)}, u32[]{:S(2)}) collective-permute-start(bf16[192,768]{1,0:T(8,128)(2,1)} %dynamic-slice_convert_fusion.4), channel_id=1, source_target_pairs={{0,16},{16,0},{1,17},{17,1},{2,18},{18,2},{3,19},{19,3},{4,20},{20... | collective-permute-start | bytes 884744 | tf_op jit(solution)/shard_map/ppermute | solution.py:286
  92.7 1.1 copy-start.1
  94.7 23.0 %collective-permute-start.21 = (bf16[192,768]{1,0:T(8,128)(2,1)}, bf16[192,768]{1,0:T(8,128)(2,1)}, u32[]{:S(2)}, u32[]{:S(2)}) collective-permute-start(bf16[192,768]{1,0:T(8,128)(2,1)} %dynamic-slice_convert_fusion.5), channel_id=1, source_target_pairs={{0,16},{16,0},{1,17},{17,1},{2,18},{18,2},{3,19},{19,3},{4,20},{20... | collective-permute-start | bytes 884744 | tf_op jit(solution)/shard_map/ppermute | solution.py:286
  95.2 40.5 %collective-permute-start.13 = (bf16[256,768]{1,0:T(8,128)(2,1)}, bf16[256,768]{1,0:T(8,128)(2,1)}, u32[]{:S(2)}, u32[]{:S(2)}) collective-permute-start(bf16[256,768]{1,0:T(8,128)(2,1)} %dynamic-slice_convert_fusion.3), channel_id=1, source_target_pairs={{0,16},{16,0},{1,17},{17,1},{2,18},{18,2},{3,19},{19,3},{4,20},{20... | collective-permute-start | bytes 1179656 | tf_op jit(solution)/shard_map/ppermute | solution.py:286
  113.4 4.3 %copy-start.4 = (f32[384,768]{1,0:T(8,128)S(1)}, f32[384,768]{1,0:T(8,128)}, u32[]{:S(2)}) copy-start(f32[384,768]{1,0:T(8,128)} %copy-done.3) | copy-start | bytes 3538948
  114.5 7.6 %collective-permute-start.30 = (bf16[96,768]{1,0:T(8,128)(2,1)S(1)}, bf16[96,768]{1,0:T(8,128)(2,1)S(1)}, u32[]{:S(2)}, u32[]{:S(2)}) collective-permute-start(bf16[96,768]{1,0:T(8,128)(2,1)S(1)} %dynamic-slice_convert_fusion.7), channel_id=1, source_target_pairs={{0,4},{2,6},{4,0},{6,2},{8,12},{10,14},{12,8},{14,10},{1,5},{3,7},... | collective-permute-start | bytes 442376 | tf_op jit(solution)/shard_map/ppermute | solution.py:286
  118.7 17.0 %copy-start.2 = (f32[512,768]{1,0:T(8,128)S(1)}, f32[512,768]{1,0:T(8,128)}, u32[]{:S(2)}) copy-start(f32[512,768]{1,0:T(8,128)} %copy-done.1) | copy-start | bytes 4718596
  118.8 7.3 %collective-permute-start.22 = (bf16[96,768]{1,0:T(8,128)(2,1)S(1)}, bf16[96,768]{1,0:T(8,128)(2,1)S(1)}, u32[]{:S(2)}, u32[]{:S(2)}) collective-permute-start(bf16[96,768]{1,0:T(8,128)(2,1)S(1)} %dynamic-slice_convert_fusion.8), channel_id=1, source_target_pairs={{0,4},{2,6},{4,0},{6,2},{8,12},{10,14},{12,8},{14,10},{1,5},{3,7},... | collective-permute-start | bytes 442376 | tf_op jit(solution)/shard_map/ppermute | solution.py:286
  122.2 10.4 %collective-permute-start.31 = (bf16[48,768]{1,0:T(8,128)(2,1)S(1)}, bf16[48,768]{1,0:T(8,128)(2,1)S(1)}, u32[]{:S(2)}, u32[]{:S(2)}) collective-permute-start(bf16[48,768]{1,0:T(8,128)(2,1)S(1)} %dynamic-slice_convert_fusion.10), channel_id=1, source_target_pairs={{0,8},{2,10},{4,12},{6,14},{8,0},{10,2},{12,4},{14,6},{1,9},{3,11}... | collective-permute-start | bytes 221192 | tf_op jit(solution)/shard_map/ppermute | solution.py:286
  126.2 8.0 %collective-permute-start.23 = (bf16[48,768]{1,0:T(8,128)(2,1)S(1)}, bf16[48,768]{1,0:T(8,128)(2,1)S(1)}, u32[]{:S(2)}, u32[]{:S(2)}) collective-permute-start(bf16[48,768]{1,0:T(8,128)(2,1)S(1)} %dynamic-slice_convert_fusion.11), channel_id=1, source_target_pairs={{0,8},{2,10},{4,12},{6,14},{8,0},{10,2},{12,4},{14,6},{1,9},{3,11}... | collective-permute-start | bytes 221192 | tf_op jit(solution)/shard_map/ppermute | solution.py:286
  132.6 6.5 %collective-permute-start.32 = (bf16[48,768]{1,0:T(8,128)(2,1)S(1)}, bf16[48,768]{1,0:T(8,128)(2,1)S(1)}, u32[]{:S(2)}, u32[]{:S(2)}) collective-permute-start(bf16[48,768]{1,0:T(8,128)(2,1)S(1)} %multiply_convert_fusion.1), channel_id=1, source_target_pairs={{0,8},{2,10},{4,12},{6,14},{8,0},{10,2},{12,4},{14,6},{1,9},{3,11}... | collective-permute-start | bytes 221192 | tf_op jit(solution)/shard_map/ppermute | solution.py:286
  134.2 5.9 %collective-permute-start.24 = (bf16[48,768]{1,0:T(8,128)(2,1)S(1)}, bf16[48,768]{1,0:T(8,128)(2,1)S(1)}, u32[]{:S(2)}, u32[]{:S(2)}) collective-permute-start(bf16[48,768]{1,0:T(8,128)(2,1)S(1)} %multiply_convert_fusion.2), channel_id=1, source_target_pairs={{0,8},{2,10},{4,12},{6,14},{8,0},{10,2},{12,4},{14,6},{1,9},{3,11}... | collective-permute-start | bytes 221192 | tf_op jit(solution)/shard_map/ppermute | solution.py:286
  136.8 9.9 %collective-permute-start.14 = (bf16[128,768]{1,0:T(8,128)(2,1)S(1)}, bf16[128,768]{1,0:T(8,128)(2,1)S(1)}, u32[]{:S(2)}, u32[]{:S(2)}) collective-permute-start(bf16[128,768]{1,0:T(8,128)(2,1)S(1)} %dynamic-slice_convert_fusion.6), channel_id=1, source_target_pairs={{0,4},{2,6},{4,0},{6,2},{8,12},{10,14},{12,8},{14,10},{1,5},{3,7},... | collective-permute-start | bytes 589832 | tf_op jit(solution)/shard_map/ppermute | solution.py:286
  139.2 6.9 %collective-permute-start.33 = (bf16[96,768]{1,0:T(8,128)(2,1)S(1)}, bf16[96,768]{1,0:T(8,128)(2,1)S(1)}, u32[]{:S(2)}, u32[]{:S(2)}) collective-permute-start(bf16[96,768]{1,0:T(8,128)(2,1)S(1)} %pad_maximum_fusion.11), channel_id=1, source_target_pairs={{0,4},{2,6},{4,0},{6,2},{8,12},{10,14},{12,8},{14,10},{1,5},{3,7},... | collective-permute-start | bytes 442376 | tf_op jit(solution)/shard_map/ppermute | solution.py:286
  140.2 7.4 %collective-permute-start.25 = (bf16[96,768]{1,0:T(8,128)(2,1)S(1)}, bf16[96,768]{1,0:T(8,128)(2,1)S(1)}, u32[]{:S(2)}, u32[]{:S(2)}) collective-permute-start(bf16[96,768]{1,0:T(8,128)(2,1)S(1)} %pad_maximum_fusion.10), channel_id=1, source_target_pairs={{0,4},{2,6},{4,0},{6,2},{8,12},{10,14},{12,8},{14,10},{1,5},{3,7},... | collective-permute-start | bytes 442376 | tf_op jit(solution)/shard_map/ppermute | solution.py:286
  146.1 14.0 %collective-permute-start.34 = (bf16[192,768]{1,0:T(8,128)(2,1)S(1)}, bf16[192,768]{1,0:T(8,128)(2,1)S(1)}, u32[]{:S(2)}, u32[]{:S(2)}) collective-permute-start(bf16[192,768]{1,0:T(8,128)(2,1)S(1)} %pad_maximum_fusion.8), channel_id=1, source_target_pairs={{0,16},{16,0},{1,17},{17,1},{2,18},{18,2},{3,19},{19,3},{4,20},{20... | collective-permute-start | bytes 884744 | tf_op jit(solution)/shard_map/ppermute | solution.py:286
  146.8 6.6 %collective-permute-start.15 = (bf16[64,768]{1,0:T(8,128)(2,1)S(1)}, bf16[64,768]{1,0:T(8,128)(2,1)S(1)}, u32[]{:S(2)}, u32[]{:S(2)}) collective-permute-start(bf16[64,768]{1,0:T(8,128)(2,1)S(1)} %dynamic-slice_convert_fusion.9), channel_id=1, source_target_pairs={{0,8},{2,10},{4,12},{6,14},{8,0},{10,2},{12,4},{14,6},{1,9},{3,11}... | collective-permute-start | bytes 294920 | tf_op jit(solution)/shard_map/ppermute | solution.py:286
  153.4 6.6 %collective-permute-start.16 = (bf16[64,768]{1,0:T(8,128)(2,1)S(1)}, bf16[64,768]{1,0:T(8,128)(2,1)S(1)}, u32[]{:S(2)}, u32[]{:S(2)}) collective-permute-start(bf16[64,768]{1,0:T(8,128)(2,1)S(1)} %multiply_convert_fusion), channel_id=1, source_target_pairs={{0,8},{2,10},{4,12},{6,14},{8,0},{10,2},{12,4},{14,6},{1,9},{3,11}... | collective-permute-start | bytes 294920 | tf_op jit(solution)/shard_map/ppermute | solution.py:286
  153.5 12.6 %collective-permute-start.26 = (bf16[192,768]{1,0:T(8,128)(2,1)S(1)}, bf16[192,768]{1,0:T(8,128)(2,1)S(1)}, u32[]{:S(2)}, u32[]{:S(2)}) collective-permute-start(bf16[192,768]{1,0:T(8,128)(2,1)S(1)} %pad_maximum_fusion.7), channel_id=1, source_target_pairs={{0,16},{16,0},{1,17},{17,1},{2,18},{18,2},{3,19},{19,3},{4,20},{20... | collective-permute-start | bytes 884744 | tf_op jit(solution)/shard_map/ppermute | solution.py:286
  160.1 5.7 %collective-permute-start.17 = (bf16[128,768]{1,0:T(8,128)(2,1)S(1)}, bf16[128,768]{1,0:T(8,128)(2,1)S(1)}, u32[]{:S(2)}, u32[]{:S(2)}) collective-permute-start(bf16[128,768]{1,0:T(8,128)(2,1)S(1)} %pad_maximum_fusion.9), channel_id=1, source_target_pairs={{0,4},{2,6},{4,0},{6,2},{8,12},{10,14},{12,8},{14,10},{1,5},{3,7},... | collective-permute-start | bytes 589832 | tf_op jit(solution)/shard_map/ppermute | solution.py:286
  165.9 7.8 %collective-permute-start.18 = (bf16[256,768]{1,0:T(8,128)(2,1)S(1)}, bf16[256,768]{1,0:T(8,128)(2,1)S(1)}, u32[]{:S(2)}, u32[]{:S(2)}) collective-permute-start(bf16[256,768]{1,0:T(8,128)(2,1)S(1)} %pad_maximum_fusion.6), channel_id=1, source_target_pairs={{0,16},{16,0},{1,17},{17,1},{2,18},{18,2},{3,19},{19,3},{4,20},{20... | collective-permute-start | bytes 1179656 | tf_op jit(solution)/shard_map/ppermute | solution.py:286
  166.0 8.0 %collective-permute-start.35 = (bf16[384,768]{1,0:T(8,128)(2,1)S(1)}, bf16[384,768]{1,0:T(8,128)(2,1)S(1)}, u32[]{:S(2)}, u32[]{:S(2)}) collective-permute-start(bf16[384,768]{1,0:T(8,128)(2,1)S(1)} %pad_maximum_fusion.5), channel_id=1, source_target_pairs={{0,2},{2,0},{4,6},{6,4},{8,10},{10,8},{12,14},{14,12},{1,3},{3,1},... | collective-permute-start | bytes 1769480 | tf_op jit(solution)/shard_map/ppermute | solution.py:286
  166.3 8.0 %collective-permute-start.27 = (bf16[384,768]{1,0:T(8,128)(2,1)S(1)}, bf16[384,768]{1,0:T(8,128)(2,1)S(1)}, u32[]{:S(2)}, u32[]{:S(2)}) collective-permute-start(bf16[384,768]{1,0:T(8,128)(2,1)S(1)} %pad_maximum_fusion.4), channel_id=1, source_target_pairs={{0,2},{2,0},{4,6},{6,4},{8,10},{10,8},{12,14},{14,12},{1,3},{3,1},... | collective-permute-start | bytes 1769480 | tf_op jit(solution)/shard_map/ppermute | solution.py:286
  174.0 3.8 %collective-permute-start.19 = (bf16[512,768]{1,0:T(8,128)(2,1)S(1)}, bf16[512,768]{1,0:T(8,128)(2,1)S(1)}, u32[]{:S(2)}, u32[]{:S(2)}) collective-permute-start(bf16[512,768]{1,0:T(8,128)(2,1)S(1)} %pad_maximum_fusion.3), channel_id=1, source_target_pairs={{0,2},{2,0},{4,6},{6,4},{8,10},{10,8},{12,14},{14,12},{1,3},{3,1},... | collective-permute-start | bytes 2359304 | tf_op jit(solution)/shard_map/ppermute | solution.py:286
